TPU v7x, 256 devices: a whole 4x4x8 slice. The times are simulated.
256 devices in a mesh: stem: 8 (over z_lo, y), tm: 32 (over x, z_hi, core).
Axes of the slice: x: 4, y: 4, z: 8 (z_hi: 4, z_lo: 2; z = z_hi * 2 + z_lo), core: 2. Of those that a mesh axis runs over, the one named last changes fastest.
Arguments:
- frames: bfloat16 [8, 12288, 1024], P('stem', 'tm'), may hold values from -6 to 6
- timestep: int32 [8], replicated, may hold values from 0 to 49, as said below
- modulation: float32 [50, 6, 1024], replicated, may hold values from -3 to 3
- qkv_self: bfloat16 [1024, 1536], replicated, may hold values from -0.1875 to 0.1875
- out_self: bfloat16 [512, 1024], replicated, may hold values from -0.25 to 0.25
- qk_gain_self: float32 [2, 64], replicated, may hold values from 1.5 to 6
- qkv_cross: bfloat16 [1024, 1536], replicated, may hold values from -0.1875 to 0.1875
- out_cross: bfloat16 [512, 1024], replicated, may hold values from -0.25 to 0.25
- qk_gain_cross: float32 [2, 64], replicated, may hold values from 1.5 to 6
Outputs:
- layer_out: bfloat16 [8, 12288, 1024], P('stem', 'tm')
Inputs may be any that keep to these rules, and one draw needn't show every extreme that they name: The stems' timestep indices are distinct, and index 0 and index 49 are always among them.
All inputs are finite; a program needn't handle non-finite values.
Results may differ from a plain program's by a relative error of at most 0.015.
The roundings to bfloat16 on the way count: a program that leaves them out, or rounds other values in their place, can miss the bound.
Values may be sent and summed in bfloat16 or wider, within the bound.
A program may use at most 128 MiB of HBM per device.

v0:
```python
import jax
import jax.numpy as jnp
from jax import lax
from jax.sharding import PartitionSpec as P

D = 1024
H = 8
HD = 64
HALF = 256


EPS = 1e-06
NEG = -1e30


def padded_2(block, sides, width):
    for axis, dim in sides:
        count = lax.axis_size(axis)
        forward = [(i, i + 1) for i in range(count - 1)]
        backward = [(target, source) for source, target in forward]
        low = lax.ppermute(
            lax.slice_in_dim(block, block.shape[dim] - width, None, axis=dim), axis, forward
        )
        high = lax.ppermute(lax.slice_in_dim(block, 0, width, axis=dim), axis, backward)
        block = jnp.concatenate([low, block, high], axis=dim)
    return block


def rounded(values):
    return lax.optimization_barrier(values.astype(jnp.bfloat16))


def layer_norm(values):
    values = values.astype(jnp.float32)
    centred = values - jnp.mean(values, axis=-1, keepdims=True)
    return centred * lax.rsqrt(jnp.mean(centred * centred, axis=-1, keepdims=True) + EPS)


def modulate(values, shift, scale):
    return layer_norm(values) * (1.0 + scale) + shift


def head_norm(values, gain):
    shaped = values.reshape(values.shape[:-1] + (H, HD))
    return shaped * lax.rsqrt(jnp.mean(shaped * shaped, axis=-1, keepdims=True) + EPS) * gain


def split_heads(projected, gains):
    width = H * HD
    query = rounded(head_norm(projected[..., :width], gains[0]))
    keyset = rounded(head_norm(projected[..., width : 2 * width], gains[1]))
    valueset = rounded(projected[..., 2 * width :].reshape(projected.shape[:-1] + (H, HD)))
    return (query, keyset, valueset)


def softmax_rows(scores):
    top = jnp.max(scores, axis=-1, keepdims=True)
    raised = jnp.exp(scores - top)
    return rounded(raised / jnp.sum(raised, axis=-1, keepdims=True))


def window_attend(query, padded, offset, total):
    rows = query.shape[0]
    width = H * HD

    def one_block(index):
        start = index * rows
        k_block = padded[0].reshape(-1, H, HD)
        v_block = padded[1].reshape(-1, H, HD)
        scores = jnp.einsum(
            "qhd,khd->hqk", query, k_block, preferred_element_type=jnp.float32
        ) * HD ** (-0.5)
        q_pos = offset + start + jnp.arange(rows, dtype=jnp.int32)
        k_pos = offset + start - HALF + jnp.arange(rows + 2 * HALF, dtype=jnp.int32)
        keep = (
            (jnp.abs(q_pos[:, None] - k_pos[None, :]) <= HALF)
            & (k_pos[None, :] >= 0)
            & (k_pos[None, :] < total)
        )
        weights = softmax_rows(jnp.where(keep[None], scores, NEG))
        return jnp.einsum("hqk,khd->qhd", weights, v_block, preferred_element_type=jnp.float32)

    blocks = lax.map(one_block, jnp.arange(rows // rows, dtype=jnp.int32))
    return rounded(blocks.reshape(rows, width))


def on_device(
    frames,
    timestep,
    modulation,
    qkv_self,
    out_self,
    qk_gain_self,
    qkv_cross,
    out_cross,
    qk_gain_cross,
):
    stem_count = lax.axis_size("stem")
    time_count = lax.axis_size("tm")
    rows = frames.shape[1]
    width = H * HD
    steps_all = modulation.shape[0]
    picks = (timestep[:, None] == jnp.arange(steps_all, dtype=jnp.int32)[None, :]).astype(
        jnp.float32
    )
    table = jnp.dot(
        picks, modulation.reshape(steps_all, -1), precision=lax.Precision.HIGHEST
    ).reshape(stem_count, 6, D)
    own = lax.dynamic_index_in_dim(table, lax.axis_index("stem"), 0, keepdims=False)
    source = frames[0]
    normed_self = rounded(modulate(source, own[0], own[1]))
    projected = jnp.dot(normed_self, qkv_self, preferred_element_type=jnp.float32)
    query, keyset, valueset = split_heads(projected, qk_gain_self)
    stacked = jnp.stack([keyset.reshape(rows, width), valueset.reshape(rows, width)])
    padded = padded_2(stacked, (("tm", 1),), HALF)
    offset = lax.axis_index("tm") * rows
    attended = window_attend(query, padded, offset, rows * time_count)
    first = rounded(
        source.astype(jnp.float32)
        + own[2] * jnp.dot(attended, out_self, preferred_element_type=jnp.float32)
    )
    normed_cross = rounded(modulate(first, own[3], own[4]))
    projected_cross = jnp.dot(normed_cross, qkv_cross, preferred_element_type=jnp.float32)
    q_cross, k_cross, v_cross = split_heads(projected_cross, qk_gain_cross)
    pair = jnp.stack([k_cross.reshape(rows, width), v_cross.reshape(rows, width)])[None]
    every = lax.all_gather(pair, "stem", axis=0, tiled=True)
    k_all = every[:, 0].reshape(stem_count, rows, H, HD)
    v_all = every[:, 1].reshape(stem_count, rows, H, HD)
    scores = jnp.einsum(
        "fhd,tfhd->fht", q_cross, k_all, preferred_element_type=jnp.float32
    ) * HD ** (-0.5)
    weights = softmax_rows(scores)
    mixed = rounded(
        jnp.einsum("fht,tfhd->fhd", weights, v_all, preferred_element_type=jnp.float32)
    ).reshape(rows, width)
    cross_out = rounded(jnp.dot(mixed, out_cross, preferred_element_type=jnp.float32))
    result = (first.astype(jnp.float32) + own[5] * cross_out.astype(jnp.float32)).astype(
        jnp.bfloat16
    )
    return result[None]


def solution(mesh):
    return jax.shard_map(
        on_device,
        mesh=mesh,
        in_specs=(P("stem", "tm", None), P(), P(), P(), P(), P(), P(), P(), P()),
        out_specs=P("stem", "tm", None),
        check_vma=False,
    )
```

profile of v0, /device:TPU:6, one launch (start us, length us, event | category | flops | bytes accessed | tf_op | source)
XLA Modules:
  0.0 175.2 jit_solution(18192869161088181082)
XLA Ops:
  6.5 2.2 %copy.46 = f32[50,6,1024]{2,1,0:T(8,128)S(1)} copy(f32[50,6,1024]{2,0,1:T(8,128)} %param.11) | data formatting | bytes 2457600 | tf_op args[2]
  8.8 0.3 pad.10
  9.0 1.9 %copy.75 = f32[7,8,6,1024]{3,1,2,0:T(8,128)} copy(f32[7,8,6,1024]{3,2,1,0:T(8,128)S(1)} %bitcast.95) | data formatting | bytes 2752512
  10.9 2.9 %dot_general.34 = f32[6,1024,50]{1,0,2:T(8,128)} reshape(f32[6144,50]{0,1:T(8,128)} %bitcast.97) | data formatting | bytes 2457600 | tf_op jit(solution)/shard_map/dot_general | solution.py:106
  13.8 1.3 convert_reduce_fusion.1
  15.1 1.5 fusion.17
  16.6 2.6 %fusion.23 = f32[8,6,1024]{2,0,1:T(8,128)S(1)} fusion(f32[6,1024,50]{1,0,2:T(8,128)} %dot_general.34, s32[8]{0:T(128)S(1)} %copy-done.10), kind=kOutput, calls=%fused_computation.35 | convolution fusion | flops 29491600 | bytes 1425440 | tf_op jit(solution)/shard_map/dot_general | solution.py:106
  19.3 1.5 fusion.20
  20.8 1.4 fusion.52
  22.2 0.1 fusion.49
  22.3 0.1 slice.123
  22.4 0.5 copy-done.8
  22.9 0.3 copy.50
  23.1 0.1 multiply_reduce_fusion.4
  23.2 0.3 copy.48
  23.5 0.1 multiply_reduce_fusion.5
  23.6 0.3 multiply_convert_fusion.2
  24.0 0.2 copy.49
  24.2 0.1 fusion.34
  24.3 7.9 %collective-permute-start.1 = (bf16[2,256,512]{1,2,0:T(8,128)(2,1)S(1)}, bf16[2,256,512]{1,2,0:T(8,128)(2,1)S(1)}, u32[]{:S(2)}, u32[]{:S(2)}) collective-permute-start(bf16[2,256,512]{1,2,0:T(8,128)(2,1)S(1)} %get-tuple-element.29), channel_id=1, source_target_pairs={{1,0},{2,1},{3,2},{4,3},{5,4},{6,5},{7,6},{8,7},{9,8},{10,9},{11,1... | collective-permute-start | bytes 1572872 | tf_op jit(solution)/shard_map/ppermute | solution.py:24
  32.2 2.1 %collective-permute-start = (bf16[2,256,512]{1,2,0:T(8,128)(2,1)S(1)}, bf16[2,256,512]{1,2,0:T(8,128)(2,1)}, u32[]{:S(2)}, u32[]{:S(2)}) collective-permute-start(bf16[2,256,512]{1,2,0:T(8,128)(2,1)S(1)} %get-tuple-element.28), channel_id=1, source_target_pairs={{0,1},{1,2},{2,3},{3,4},{4,5},{5,6},{6,7},{7,8},{8,9},{9,10},{10,1... | collective-permute-start | bytes 1572872 | tf_op jit(solution)/shard_map/ppermute | solution.py:21
  34.4 0.6 slice_bitcast_fusion.1
  34.9 1.2 fusion.26
  36.2 8.3 %collective-permute-done.1 = bf16[2,256,512]{1,2,0:T(8,128)(2,1)S(1)} collective-permute-done((bf16[2,256,512]{1,2,0:T(8,128)(2,1)S(1)}, bf16[2,256,512]{1,2,0:T(8,128)(2,1)S(1)}, u32[]{:S(2)}, u32[]{:S(2)}) %collective-permute-start.1) | collective-permute-done | bytes 524320 | tf_op jit(solution)/shard_map/ppermute | solution.py:24
  44.5 6.3 %collective-permute-done = bf16[2,256,512]{1,2,0:T(8,128)(2,1)} collective-permute-done((bf16[2,256,512]{1,2,0:T(8,128)(2,1)S(1)}, bf16[2,256,512]{1,2,0:T(8,128)(2,1)}, u32[]{:S(2)}, u32[]{:S(2)}) %collective-permute-start) | collective-permute-done | bytes 524320 | tf_op jit(solution)/shard_map/ppermute | solution.py:21
  50.8 1.2 pad_maximum_fusion
  52.0 0.0 copy-start.5
  52.0 1.1 fusion.50
  53.1 9.1 %fusion.51 = (f32[8,384]{1,0:T(8,128)S(1)}, f32[8,384,896]{2,1,0:T(8,128)}) fusion(pred[384,896]{1,0:T(8,128)(4,1)S(1)} %copy-done.5, bf16[384,8,64]{0,2,1:T(8,128)(2,1)S(1)} %get-tuple-element.42, bf16[896,8,64]{0,2,1:T(8,128)(2,1)} %bitcast.105), kind=kOutput, calls=%fused_computation.98 | convolution fusion | flops 363332480 | bytes 12677120 | tf_op jit(solution)/shard_map/while/body/eval_jaxpr/sub | solution.py:58
  62.2 5.0 %divide_convert_fusion = bf16[8,384,896]{2,1,0:T(8,128)(2,1)S(1)} fusion(f32[8,384,896]{2,1,0:T(8,128)} %get-tuple-element.41, f32[8,384]{1,0:T(8,128)S(1)} %get-tuple-element.40), kind=kLoop, calls=%fused_computation.3 | loop fusion | flops 5505024 | bytes 16527360 | tf_op jit(solution)/shard_map/while/body/eval_jaxpr/convert_element_type | solution.py:30
  67.3 1.9 %convolution_convert_fusion.1 = bf16[8,64,384]{2,1,0:T(8,128)(2,1)S(1)} fusion(bf16[896,8,64]{0,2,1:T(8,128)(2,1)S(1)} %bitcast.98, bf16[8,384,896]{2,1,0:T(8,128)(2,1)S(1)} %divide_convert_fusion), kind=kOutput, calls=%fused_computation.40 | convolution fusion | flops 352518144 | bytes 6815744 | tf_op jit(solution)/shard_map/while/body/eval_jaxpr/hqk,khd->qhd/dot_general | solution.py:81
  69.2 0.6 fusion.21
  69.8 0.2 convert_reduce_fusion
  70.0 0.3 fusion.13
  70.4 0.4 copy-done.2
  70.8 0.4 fusion.16
  71.1 0.9 copy-done.11
  72.0 1.4 fusion.53
  73.4 0.1 slice.122
  73.5 0.1 fusion.48
  73.6 0.2 copy.53
  73.8 0.3 copy.52
  74.1 0.1 multiply_reduce_fusion.2
  74.2 0.0 copy-done.7
  74.2 0.1 multiply_convert_fusion
  74.4 0.1 pad_maximum_fusion.1
  74.5 1.2 copy.54
  75.7 0.0 all-gather.3.cloned.1.call-update
  75.7 0.3 copy.51
  76.0 0.1 multiply_reduce_fusion.3
  76.1 0.3 copy-done.6
  76.3 0.1 multiply_convert_fusion.1
  76.5 0.9 convert.8
  77.4 70.4 %all-gather.3.cloned.1.call-done = bf16[16,384,512]{2,1,0:T(8,128)(2,1)} async-done(((bf16[2,384,512]{2,1,0:T(8,128)(2,1)}), bf16[16,384,512]{2,1,0:T(8,128)(2,1)}) %all-gather.3.cloned.1.call-update) | async-done | bytes 6291472 | tf_op jit(solution)/shard_map/all_gather | solution.py:126
  147.9 6.1 %fusion.47 = (bf16[8,1,384,512]{3,2,1,0:T(8,128)(2,1)}, bf16[8,1,384,512]{3,2,1,0:T(8,128)(2,1)}) fusion(bf16[8,2,384,512]{3,2,1,0:T(8,128)(2,1)} %bitcast.96), kind=kLoop, calls=%fused_computation.94 | loop fusion | bytes 12582912 | tf_op jit(solution)/shard_map/slice | solution.py:127
  153.9 3.4 %copy.71 = bf16[8,1,384,512]{2,3,0,1:T(8,128)(2,1)S(1)} copy(bf16[8,1,384,512]{3,2,1,0:T(8,128)(2,1)} %get-tuple-element.14) | data formatting | bytes 6291456
  157.4 4.6 %copy.70 = bf16[8,1,384,512]{2,3,0,1:T(8,128)(2,1)} copy(bf16[8,1,384,512]{3,2,1,0:T(8,128)(2,1)} %get-tuple-element.13) | data formatting | bytes 6291456
  162.0 3.1 %multiply_reduce_fusion.1 = f32[384,8,8]{0,1,2:T(8,128)S(1)} fusion(bf16[384,8,64,8]{0,2,1,3:T(8,128)(2,1)} %bitcast.94, f32[384,8,64]{0,2,1:T(8,128)} %convert.8), kind=kLoop, calls=%fused_computation.8 | loop fusion | flops 4694016 | bytes 4030464
  165.1 0.1 fusion.32
  165.2 0.8 multiply_reduce_fusion
  166.0 0.4 copy-done.13
  166.4 0.6 convolution_convert_fusion
  167.0 0.2 copy-done.3
  167.2 1.2 fusion.33
  (35 shorter events, 0.2 us)
Async XLA Ops:
  6.5 14.2 %copy-start = (bf16[1024,1536]{1,0:T(8,128)(2,1)S(1)}, bf16[1024,1536]{1,0:T(8,128)(2,1)}, u32[]{:S(2)}) copy-start(bf16[1024,1536]{1,0:T(8,128)(2,1)} %param.12) | copy-start | bytes 9437188
  6.5 141.3 %all-gather.3.cloned.1.call-start = ((), (), s32[]{:S(2)}) async-start(), calls=%async_computation | async-start | bytes 7077888 | tf_op jit(solution)/shard_map/all_gather | solution.py:126
  10.9 5.7 %copy-start.10 = (s32[8]{0:T(128)S(1)}, s32[8]{0:T(128)}, u32[]{:S(2)}) copy-start(s32[8]{0:T(128)} %param.10) | copy-start | bytes 100
  22.2 0.7 copy-start.8
  24.0 10.4 %copy-start.9 = (f32[2,64]{1,0:T(2,128)S(1)}, f32[2,64]{1,0:T(2,128)}, u32[]{:S(2)}) copy-start(f32[2,64]{1,0:T(2,128)} %param.17) | copy-start | bytes 1540
  24.3 20.2 %collective-permute-start.1 = (bf16[2,256,512]{1,2,0:T(8,128)(2,1)S(1)}, bf16[2,256,512]{1,2,0:T(8,128)(2,1)S(1)}, u32[]{:S(2)}, u32[]{:S(2)}) collective-permute-start(bf16[2,256,512]{1,2,0:T(8,128)(2,1)S(1)} %get-tuple-element.29), channel_id=1, source_target_pairs={{1,0},{2,1},{3,2},{4,3},{5,4},{6,5},{7,6},{8,7},{9,8},{10,9},{11,1... | collective-permute-start | bytes 1572872 | tf_op jit(solution)/shard_map/ppermute | solution.py:24
  32.2 18.6 %collective-permute-start = (bf16[2,256,512]{1,2,0:T(8,128)(2,1)S(1)}, bf16[2,256,512]{1,2,0:T(8,128)(2,1)}, u32[]{:S(2)}, u32[]{:S(2)}) collective-permute-start(bf16[2,256,512]{1,2,0:T(8,128)(2,1)S(1)} %get-tuple-element.28), channel_id=1, source_target_pairs={{0,1},{1,2},{2,3},{3,4},{4,5},{5,6},{6,7},{7,8},{8,9},{9,10},{10,1... | collective-permute-start | bytes 1572872 | tf_op jit(solution)/shard_map/ppermute | solution.py:21
  52.0 1.1 copy-start.5
  67.3 1.9 %copy-start.4 = (bf16[1,384,1024]{2,1,0:T(8,128)(2,1)S(1)}, bf16[1,384,1024]{2,1,0:T(8,128)(2,1)}, u32[]{:S(2)}) copy-start(bf16[1,384,1024]{2,1,0:T(8,128)(2,1)} %param.9) | copy-start | bytes 2359300
  67.3 1.9 %copy-start.12 = (bf16[512,1024]{1,0:T(8,128)(2,1)S(1)}, bf16[512,1024]{1,0:T(8,128)(2,1)}, u32[]{:S(2)}) copy-start(bf16[512,1024]{1,0:T(8,128)(2,1)} %param.13) | copy-start | bytes 3145732
  69.8 0.9 copy-start.2
  69.8 2.2 %copy-start.11 = (bf16[1024,1536]{1,0:T(8,128)(2,1)S(1)}, bf16[1024,1536]{1,0:T(8,128)(2,1)}, u32[]{:S(2)}) copy-start(bf16[1024,1536]{1,0:T(8,128)(2,1)} %param.15) | copy-start | bytes 9437188
  73.6 0.6 copy-start.7
  75.7 0.7 copy-start.6
  165.2 1.2 copy-start.13
  166.0 1.2 copy-start.3
  166.0 2.4 %copy-start.1 = (bf16[1024,1536]{1,0:T(8,128)(2,1)S(1)}, bf16[1024,1536]{1,0:T(8,128)(2,1)}, u32[]{:S(2)}) copy-start(bf16[1024,1536]{1,0:T(8,128)(2,1)} %param.12) | copy-start | bytes 9437188
Sparse Core Ops, SparseCore 0:
  75.8 72.0 all-gather.2
where the time goes:
time: 177 us; the launch traced here: 175 us
  waiting for transfers between devices  85 us (48%)
  local copies, waits for them, and re-layouts  28.8 us (16%)
  other arithmetic  19.9 us (11%)
  matrix products  17.6 us (10%)
  between operations  13.9 us (8%)
  starting transfers between devices  10 us (6%)
    all_gather x1, waiting for transfers between devices, on_device(): every = lax.all_gather(pair, 'stem', axis=0, tiled=True)  70.4 us
    unnamed x34, local copies, waits for them, and re-layouts  15.1 us
    sub x1, matrix products, softmax_rows(): raised = jnp.exp(scores - top)  9.13 us
    ppermute x1, waiting for transfers between devices, padded_2(): lax.ppermute(lax.slice_in_dim(block, 0, width, axis=dim), axis, backward)  8.34 us
    ppermute x1, starting transfers between devices, padded_2(): lax.ppermute(lax.slice_in_dim(block, 0, width, axis=dim), axis, backward)  7.91 us
    convert_element_type x6, other arithmetic, rounded(): return lax.optimization_barrier(values.astype(jnp.bfloat16))  7.51 us
    ppermute x1, waiting for transfers between devices, padded_2(): lax.ppermute(lax.slice_in_dim(block, block.shape[dim] - width, None, axis...  6.25 us
    slice x1, local copies, waits for them, and re-layouts, on_device(): k_all = every[:, 0].reshape(stem_count, rows, H, HD)  6.06 us
  transfers between devices with their start and end apart: 3, of which 3 were waited for; matrix products, arithmetic and copies ran while one was open for 2% of the time, Pallas kernels for 0%

commit v1 on v0

v1 whole, which is shorter than its diff:
```python
import jax
import jax.numpy as jnp
from jax import lax
from jax.experimental import pallas as pl
from jax.experimental.pallas import tpu as pltpu
from jax.sharding import PartitionSpec as P

HD = 64
EPS = 1e-06
NEG = -1e30
BLK = 128
F32 = jnp.float32
BF16 = jnp.bfloat16
MESH = pl.DeviceIdType.MESH


def matmul(a, b):
    return jnp.dot(a, b, preferred_element_type=F32)


def matmul_nt(a, b):
    return lax.dot_general(a, b, (((1,), (1,)), ((), ())), preferred_element_type=F32)


def make_kernel(stems, tms, steps, rows, width, hw):
    blocks = rows // BLK
    part = BLK // stems
    pairs = hw // 128

    def kernel(
        frames_hbm, timestep_hbm, mod_hbm, w1_hbm, wo1_hbm, g1_hbm, w2_hbm, wo2_hbm, g2_hbm,
        out_hbm,
        x_buf, t_smem, mod_buf, w1, wo1, g1, w2, wo2, g2, gains, diag,
        norm_buf, q_buf, kv_buf, m_buf, o_buf, attn_buf,
        first_buf, recv_buf, cmix_buf, recv2_buf, out_buf,
        load_sem, store_sem, hs_sem, hr_sem, as_sem, ar_sem, bs_sem, br_sem,
    ):
        me_s = lax.axis_index("stem")
        me_t = lax.axis_index("tm")
        left, right = me_t - 1, me_t + 1
        half = stems // 2
        me_hi, me_lo = me_s // half, lax.rem(me_s, half)
        peers = [
            lax.rem(me_hi + r // half, 2) * half + lax.rem(me_lo + r % half, half)
            for r in range(stems)
        ]
        order = list(range(half, stems)) + list(range(1, half))
        has_left, has_right = me_t > 0, me_t < tms - 1

        loads = [
            pltpu.make_async_copy(src, dst, load_sem.at[i])
            for i, (src, dst) in enumerate([
                (timestep_hbm, t_smem), (frames_hbm, x_buf.at[pl.ds(2 * BLK, rows), :]),
                (mod_hbm, mod_buf), (w1_hbm, w1),
                (g1_hbm, g1), (g2_hbm, g2), (wo1_hbm, wo1), (w2_hbm, w2), (wo2_hbm, wo2),
            ])
        ]
        barrier = pltpu.get_barrier_semaphore()

        def greet(to):
            pl.semaphore_signal(barrier, inc=1, device_id=to, device_id_type=MESH)

        for r in order:
            greet({"stem": peers[r]})

        @pl.when(has_left)
        def _():
            greet({"tm": left})

        @pl.when(has_right)
        def _():
            greet({"tm": right})

        for load in loads:
            load.start()

        def halo_copy(index, source_block, target_block, to):
            return pltpu.make_async_remote_copy(
                src_ref=frames_hbm.at[pl.ds(source_block * BLK, BLK), :],
                dst_ref=x_buf.at[pl.ds(target_block * BLK, BLK), :],
                send_sem=hs_sem.at[index],
                recv_sem=hr_sem.at[index],
                device_id={"tm": to},
                device_id_type=MESH,
            )

        to_left = [halo_copy(0, 0, 5, left), halo_copy(2, 1, 6, left)]
        to_right = [halo_copy(1, 2, 1, right), halo_copy(3, 1, 0, right)]

        pl.semaphore_wait(
            barrier, stems - 1 + has_left.astype(jnp.int32) + has_right.astype(jnp.int32)
        )
        for step in range(2):
            pl.when(has_left)(to_left[step].start)
            pl.when(has_right)(to_right[step].start)

        @pl.when(jnp.logical_not(has_left))
        def _():
            x_buf[0 : 2 * BLK, :] = jnp.zeros((2 * BLK, width), BF16)

        @pl.when(jnp.logical_not(has_right))
        def _():
            x_buf[rows + 2 * BLK :, :] = jnp.zeros((2 * BLK, width), BF16)

        def halo_arrived(step):
            pl.when(has_right)(to_left[step].wait_recv)
            pl.when(has_left)(to_right[step].wait_recv)

        row = lax.broadcasted_iota(jnp.int32, (256, 256), 0)
        col = lax.broadcasted_iota(jnp.int32, (256, 256), 1)
        diag[...] = jnp.where((row >> 6) == (col >> 6), 1.0 / HD, 0.0).astype(BF16)

        loads[4].wait()
        loads[5].wait()
        for i, g in enumerate((g1, g2)):
            two = jnp.concatenate([g[...], g[...]], axis=1)
            wide = jnp.concatenate([two] * pairs, axis=1)
            gains[2 * i : 2 * i + 1, :] = wide[0:1] * (HD ** -0.5)
            gains[2 * i + 1 : 2 * i + 2, :] = wide[1:2]

        def normed(values, shift, scale):
            values = values.astype(F32)
            centred = values - jnp.mean(values, axis=-1, keepdims=True)
            var = jnp.mean(centred * centred, axis=-1, keepdims=True)
            return (centred * lax.rsqrt(var + EPS) * scale + shift).astype(BF16)

        def head_norm(values, gain):
            square = (values * values).astype(BF16)
            mean = jnp.concatenate(
                [matmul(square[:, i : i + 256], diag[...]) for i in range(0, hw, 256)], axis=1
            )
            return (values * lax.rsqrt(mean + EPS) * gain).astype(BF16)

        loads[0].wait()
        loads[1].wait()
        loads[2].wait()
        t_own = t_smem[me_s]

        def mods(which, at):
            return mod_buf[which, pl.ds(at, 1), :]

        shift1, scale1 = mods(0, t_own), mods(1, t_own) + 1.0

        def norm_rows(i, carry):
            at = pl.ds(pl.multiple_of(i * 32, 32), 32)
            norm_buf[at, :] = normed(x_buf[at, :], shift1, scale1)
            return carry

        def norm_blocks(first, last):
            lax.fori_loop(first * (BLK // 32), last * (BLK // 32), norm_rows, 0)

        def key_values(block):
            at = pl.ds(block * BLK, BLK)
            keys = matmul(norm_buf[at, :], w1[:, hw : 2 * hw])
            kv_buf[0, at, :] = head_norm(keys, gains[1:2, :])
            kv_buf[1, at, :] = matmul(norm_buf[at, :], w1[:, 2 * hw :]).astype(BF16)

        norm_blocks(2, 5)
        loads[3].wait()
        for block in (2, 3, 4):
            key_values(block)
        for block in range(blocks):
            at = pl.ds((2 + block) * BLK, BLK)
            q_buf[pl.ds(block * BLK, BLK), :] = head_norm(
                matmul(norm_buf[at, :], w1[:, :hw]), gains[0:1, :]
            )

        r_at = lax.broadcasted_iota(jnp.int32, (2 * BLK, BLK), 0) & (BLK - 1)
        c_at = lax.broadcasted_iota(jnp.int32, (2 * BLK, BLK), 1)
        low_lanes = lax.broadcasted_iota(jnp.int32, (BLK, 128), 1) < HD
        bias_left = jnp.where(me_t == 0, NEG, 0.0).astype(F32)
        bias_right = jnp.where(me_t == tms - 1, NEG, 0.0).astype(F32)

        def two_heads(q):
            zero = jnp.zeros_like(q)
            return jnp.concatenate(
                [jnp.where(low_lanes, q, zero), jnp.where(low_lanes, zero, q)], axis=0
            )

        def with_ones(v):
            return jnp.concatenate([v, jnp.ones_like(v)], axis=1)

        def keep(scores, kind):
            if kind == -1:
                return jnp.where(c_at >= r_at, scores, NEG)
            if kind == 1:
                return jnp.where(c_at <= r_at, scores, NEG)
            return scores

        def pieces(block, pair, spans):
            lanes = pl.ds(pair * 128, 128)
            q2 = two_heads(q_buf[pl.ds(block * BLK, BLK), lanes])
            scores, values = [], []
            for start, kind, bias in spans:
                at = pl.ds(start * BLK, BLK)
                part_scores = matmul_nt(q2, kv_buf[0, at, lanes])
                if bias is not None:
                    part_scores = part_scores + bias
                scores.append(keep(part_scores, kind))
                values.append(with_ones(kv_buf[1, at, lanes]))
            return jnp.concatenate(scores, axis=1), jnp.concatenate(values, axis=0)

        own_spans = {
            0: [(2, 0, None), (3, 0, None), (4, 1, None)],
            1: [(2, 0, None), (3, 0, None), (4, 0, None)],
            2: [(2, -1, None), (3, 0, None), (4, 0, None)],
        }
        halo_spans = {
            0: [(0, -1, bias_left), (1, 0, bias_left)],
            1: [(1, -1, bias_left), (5, 1, bias_right)],
            2: [(5, 0, bias_right), (6, 1, bias_right)],
        }

        def own_part(block):
            for pair in range(pairs):
                scores, values = pieces(block, pair, own_spans[block])
                top = jnp.max(scores, axis=-1, keepdims=True)
                raised = jnp.exp(scores - top).astype(BF16)
                m_buf[block, pair] = jnp.broadcast_to(top, (2 * BLK, 128))
                o_buf[block, pair] = matmul(raised, values)

        def halo_part(block):
            for pair in range(pairs):
                scores, values = pieces(block, pair, halo_spans[block])
                before = m_buf[block, pair][:, 0:1]
                top = jnp.maximum(before, jnp.max(scores, axis=-1, keepdims=True))
                raised = jnp.exp(scores - top).astype(BF16)
                total = o_buf[block, pair] * jnp.exp(before - top) + matmul(raised, values)
                mixed = total[:, :128] / total[:, 128:]
                both = jnp.where(low_lanes, mixed[:BLK], mixed[BLK:])
                attn_buf[:, pl.ds(pair * 128, 128)] = both.astype(BF16)

        gate1 = mods(2, t_own)

        def first_copy(block, r):
            return pltpu.make_async_remote_copy(
                src_ref=first_buf.at[block, peers[r]],
                dst_ref=recv_buf.at[block, me_s],
                send_sem=as_sem.at[block, r],
                recv_sem=ar_sem.at[block, r],
                device_id={"stem": peers[r]},
                device_id_type=MESH,
            )

        def home_copy(block, r):
            return pltpu.make_async_remote_copy(
                src_ref=cmix_buf.at[block, peers[r]],
                dst_ref=recv2_buf.at[block, me_s],
                send_sem=bs_sem.at[block, r],
                recv_sem=br_sem.at[block, r],
                device_id={"stem": peers[r]},
                device_id_type=MESH,
            )

        def first_part(block):
            at = pl.ds((2 + block) * BLK, BLK)
            value = x_buf[at, :].astype(F32) + gate1 * matmul(attn_buf[...], wo1[...])
            first_buf[block] = value.astype(BF16).reshape(stems, part, width)
            recv_buf[block, me_s] = first_buf[block, me_s]
            for r in order:
                first_copy(block, r).start()

        def cross_part(block):
            for r in order:
                first_copy(block, r).wait_recv()
            for s in range(stems):
                norm_buf[s * part : (s + 1) * part, :] = normed(
                    recv_buf[block, s], mods(3, t_smem[s]), mods(4, t_smem[s]) + 1.0
                )
            rows_in = norm_buf[0:BLK, :]
            q = head_norm(matmul(rows_in, w2[:, :hw]), gains[2:3, :])
            k = head_norm(matmul(rows_in, w2[:, hw : 2 * hw]), gains[3:4, :])
            v = matmul(rows_in, w2[:, 2 * hw :]).astype(BF16)
            same = (r_at & (part - 1)) == (c_at & (part - 1))
            for pair in range(pairs):
                lanes = slice(pair * 128, pair * 128 + 128)
                scores = jnp.where(same, matmul_nt(two_heads(q[:, lanes]), k[:, lanes]), NEG)
                top = jnp.max(scores, axis=-1, keepdims=True)
                raised = jnp.exp(scores - top).astype(BF16)
                total = matmul(raised, with_ones(v[:, lanes]))
                mixed = total[:, :128] / total[:, 128:]
                both = jnp.where(low_lanes, mixed[:BLK], mixed[BLK:]).astype(BF16)
                cmix_buf[block, :, :, lanes] = both.reshape(stems, part, 128)
            recv2_buf[block, me_s] = cmix_buf[block, me_s]
            for r in order:
                home_copy(block, r).start()

        gate2 = mods(5, t_own)

        def last_part(block):
            for r in order:
                home_copy(block, r).wait_recv()
            cross = matmul(recv2_buf[block].reshape(BLK, hw), wo2[...]).astype(BF16).astype(F32)
            first = first_buf[block].reshape(BLK, width).astype(F32)
            out_buf[pl.ds(block * BLK, BLK), :] = (first + gate2 * cross).astype(BF16)
            store(block).start()

        def store(block):
            at = pl.ds(block * BLK, BLK)
            return pltpu.make_async_copy(out_buf.at[at, :], out_hbm.at[at, :], store_sem.at[block])

        for block in (1, 0, 2):
            own_part(block)
        loads[6].wait()
        halo_arrived(0)
        for block in (1, 5):
            norm_blocks(block, block + 1)
            key_values(block)
        halo_part(1)
        first_part(1)
        halo_arrived(1)
        for block, halo in ((0, 0), (2, 6)):
            norm_blocks(halo, halo + 1)
            key_values(halo)
            halo_part(block)
            first_part(block)
        loads[7].wait()
        for block in (1, 0, 2):
            cross_part(block)
        loads[8].wait()
        for block in (1, 0, 2):
            last_part(block)

        for step in range(2):
            pl.when(has_left)(to_left[step].wait_send)
            pl.when(has_right)(to_right[step].wait_send)
        for block in (1, 0, 2):
            for r in order:
                first_copy(block, r).wait_send()
                home_copy(block, r).wait_send()
            store(block).wait()

    return kernel


def solution(mesh):
    stems, tms = mesh.shape["stem"], mesh.shape["tm"]

    def on_device(
        frames, timestep, modulation, qkv_self, out_self, gain_self, qkv_cross, out_cross, gain_cross
    ):
        rows, width = frames.shape[1:]
        hw = out_self.shape[0]
        steps = modulation.shape[0]
        blocks, part, pairs = rows // BLK, BLK // stems, hw // 128
        result = pl.pallas_call(
            make_kernel(stems, tms, steps, rows, width, hw),
            out_shape=jax.ShapeDtypeStruct((rows, width), BF16),
            in_specs=[pl.BlockSpec(memory_space=pl.ANY)] * 9,
            out_specs=pl.BlockSpec(memory_space=pl.ANY),
            scratch_shapes=[
                pltpu.VMEM((rows + 4 * BLK, width), BF16),
                pltpu.SMEM((stems,), jnp.int32),
                pltpu.VMEM((6, steps, width), F32),
                pltpu.VMEM((width, 3 * hw), BF16),
                pltpu.VMEM((hw, width), BF16),
                pltpu.VMEM((2, HD), F32),
                pltpu.VMEM((width, 3 * hw), BF16),
                pltpu.VMEM((hw, width), BF16),
                pltpu.VMEM((2, HD), F32),
                pltpu.VMEM((4, hw), F32),
                pltpu.VMEM((256, 256), BF16),
                pltpu.VMEM((rows + 4 * BLK, width), BF16),
                pltpu.VMEM((rows, hw), BF16),
                pltpu.VMEM((2, rows + 4 * BLK, hw), BF16),
                pltpu.VMEM((blocks, pairs, 2 * BLK, 128), F32),
                pltpu.VMEM((blocks, pairs, 2 * BLK, 256), F32),
                pltpu.VMEM((BLK, hw), BF16),
                pltpu.VMEM((blocks, stems, part, width), BF16),
                pltpu.VMEM((blocks, stems, part, width), BF16),
                pltpu.VMEM((blocks, stems, part, hw), BF16),
                pltpu.VMEM((blocks, stems, part, hw), BF16),
                pltpu.VMEM((rows, width), BF16),
                pltpu.SemaphoreType.DMA((9,)),
                pltpu.SemaphoreType.DMA((blocks,)),
                pltpu.SemaphoreType.DMA((4,)),
                pltpu.SemaphoreType.DMA((4,)),
                pltpu.SemaphoreType.DMA((blocks, stems)),
                pltpu.SemaphoreType.DMA((blocks, stems)),
                pltpu.SemaphoreType.DMA((blocks, stems)),
                pltpu.SemaphoreType.DMA((blocks, stems)),
            ],
            compiler_params=pltpu.CompilerParams(
                collective_id=0, has_side_effects=True, vmem_limit_bytes=60 << 20
            ),
            name="block",
        )(
            frames.reshape(rows, width), timestep, modulation.transpose(1, 0, 2), qkv_self, out_self, gain_self,
            qkv_cross, out_cross, gain_cross,
        )
        return result[None]

    return jax.shard_map(
        on_device,
        mesh=mesh,
        in_specs=(P("stem", "tm", None), P(), P(), P(), P(), P(), P(), P(), P()),
        out_specs=P("stem", "tm", None),
        check_vma=False,
    )
```

time: 177 us -> 44.5 us (0.25)
  waiting for transfers between devices: 85 us -> 0 us
  Pallas kernels: 0 us -> 42.3 us
  local copies, waits for them, and re-layouts: 28.8 us -> 2.06 us
  other arithmetic: 19.9 us -> 0 us
  matrix products: 17.6 us -> 0 us
  between operations: 13.9 us -> 0.01 us
  starting transfers between devices: 10 us -> 0 us
    all_gather x1 -> x0, waiting for transfers between devices: 70.4 us -> none  [on_device(): every = lax.all_gather(pair, 'stem', axis=0, tiled=True)]
    pallas_call x0 -> x1, Pallas kernels: none -> 42.3 us  [on_device(): pl.pallas_call(make_kernel(stems, tms, steps, rows, width, hw), out_shape...]
    ppermute x2 -> x0, waiting for transfers between devices: 14.6 us -> none  [the longest x1 8.34 us: padded_2(): lax.ppermute(lax.slice_in_dim(block, 0, width, axis=dim), axis, backward)]
    unnamed x34 -> x1, local copies, waits for them, and re-layouts: 15.1 us -> 2.06 us
    ppermute x2 -> x0, starting transfers between devices: 10 us -> none  [the longest x1 7.91 us: padded_2(): lax.ppermute(lax.slice_in_dim(block, 0, width, axis=dim), axis, backward)]
    sub x1 -> x0, matrix products: 9.13 us -> none  [softmax_rows(): raised = jnp.exp(scores - top)]
    slice x12 -> x0, local copies, waits for them, and re-layouts: 8.96 us -> none  [the longest x1 6.06 us: on_device(): k_all = every[:, 0].reshape(stem_count, rows, H, HD)]
    dot_general x6 -> x0, matrix products: 8.49 us -> none  [the longest x1 2.61 us: on_device(): jnp.dot(picks, modulation.reshape(steps_all, -1), precision=lax.Precision...]
  transfers between devices with their start and end apart: 3 -> 0, of which waited for: 3 -> 0; matrix products, arithmetic and copies ran while one was open for 2% -> 0% of each run, Pallas kernels for 0% -> 0%
where the time goes in v1:
time: 44.5 us; the launch traced here: 44.4 us
  Pallas kernels  42.3 us (95%)
  local copies, waits for them, and re-layouts  2.06 us (5%)
    pallas_call x1, Pallas kernels, on_device(): pl.pallas_call(make_kernel(stems, tms, steps, rows, width, hw), out_shape...  42.3 us
    unnamed x1, local copies, waits for them, and re-layouts  2.06 us

profile of v1, /device:TPU:6, one launch (start us, length us, event | category | flops | bytes accessed | tf_op | source)
XLA Modules:
  0.0 44.4 jit_solution(17644872141771015764)
XLA Ops:
  0.0 42.3 %block.1 = bf16[384,1024]{1,0:T(8,128)(2,1)} custom-call(bf16[384,1024]{1,0:T(8,128)(2,1)} %bitcast.5, s32[8]{0:T(128)} %timestep_hbm.1, f32[6,50,1024]{2,1,0:T(8,128)} %bitcast.4, bf16[1024,1536]{1,0:T(8,128)(2,1)} %w1_hbm.1, bf16[512,1024]{1,0:T(8,128)(2,1)} %wo1_hbm.1, f32[2,64]{1,0:T(2,128)} %g1_hbm.1, bf16[1024,1536]{1,0:T(8,128)(2,1)} %w2_hbm.1, ...), custom_call_target="tpu_custom_call" | custom-call | tf_op jit(solution)/shard_map/block/pallas_call | solution.py:346
  42.4 2.1 %copy.11 = bf16[1,384,1024]{2,1,0:T(8,128)(2,1)} copy(bf16[1,384,1024]{2,1,0:T(8,128)(2,1)} %bitcast.3) | data formatting | bytes 1572864

commit v2 on v1

v2 whole, which is shorter than its diff:
```python
import jax
import jax.numpy as jnp
from jax import lax
from jax.experimental import pallas as pl
from jax.experimental.pallas import tpu as pltpu
from jax.sharding import PartitionSpec as P

HD = 64
EPS = 1e-06
NEG = -1e30
BLK = 128
F32 = jnp.float32
BF16 = jnp.bfloat16
MESH = pl.DeviceIdType.MESH


def matmul(a, b):
    return jnp.dot(a, b, preferred_element_type=F32)


def matmul_nt(a, b):
    return lax.dot_general(a, b, (((1,), (1,)), ((), ())), preferred_element_type=F32)


def make_kernel(stems, tms, steps, rows, width, hw):
    blocks = rows // BLK
    part = BLK // stems
    pairs = hw // 128

    def kernel(
        frames_hbm, timestep_hbm, mod_hbm, w1_hbm, wo1_hbm, g1_hbm, w2_hbm, wo2_hbm, g2_hbm,
        out_hbm,
        x_buf, t_smem, mod_buf, w1, wo1, g1, w2, wo2, g2, gains, diag,
        norm_buf, q_buf, kv_buf, m_buf, o_buf, e_buf, attn_buf, back_buf, got_buf, back_lse, got_lse,
        first_buf, recv_buf, cmix_buf, recv2_buf, out_buf,
        load_sem, store_sem, hs_sem, hr_sem, as_sem, ar_sem, bs_sem, br_sem,
    ):
        me_s = lax.axis_index("stem")
        me_t = lax.axis_index("tm")
        odd = lax.rem(me_t, 2)
        beyond, partner = me_t - 1 + 2 * odd, me_t + 1 - 2 * odd
        has_beyond = jnp.logical_and(beyond >= 0, beyond < tms)

        def rows_of(block):
            place = block + odd * (blocks - 1 - 2 * block)
            return pl.ds(pl.multiple_of(place * BLK, BLK), BLK)

        half = stems // 2
        me_hi, me_lo = me_s // half, lax.rem(me_s, half)
        peers = [
            lax.rem(me_hi + r // half, 2) * half + lax.rem(me_lo + r % half, half)
            for r in range(stems)
        ]
        order = list(range(half, stems)) + list(range(1, half))

        loads = [
            pltpu.make_async_copy(src, dst, load_sem.at[i])
            for i, (src, dst) in enumerate([
                (timestep_hbm, t_smem), (mod_hbm, mod_buf), (g1_hbm, g1), (g2_hbm, g2),
                (w1_hbm, w1), (wo1_hbm, wo1), (w2_hbm, w2), (wo2_hbm, wo2),
            ])
        ]
        barrier = pltpu.get_barrier_semaphore()

        def greet(to):
            pl.semaphore_signal(barrier, inc=1, device_id=to, device_id_type=MESH)

        for r in order:
            greet({"stem": peers[r]})

        greet({"tm": partner})

        @pl.when(has_beyond)
        def _():
            greet({"tm": beyond})

        own_loads = [
            pltpu.make_async_copy(
                frames_hbm.at[rows_of(block), :],
                x_buf.at[pl.ds((2 + block) * BLK, BLK), :],
                load_sem.at[8 + block],
            )
            for block in range(blocks)
        ]
        loads[0].start()
        for load in own_loads:
            load.start()
        for load in loads[1:]:
            load.start()

        def near_copy(index, block, slot, to):
            return pltpu.make_async_remote_copy(
                src_ref=frames_hbm.at[rows_of(block), :],
                dst_ref=x_buf.at[pl.ds(slot * BLK, BLK), :],
                send_sem=hs_sem.at[index],
                recv_sem=hr_sem.at[index],
                device_id={"tm": to},
                device_id_type=MESH,
            )

        def far_copy(index, slot, to):
            return pltpu.make_async_remote_copy(
                src_ref=kv_buf.at[:, pl.ds(3 * BLK, BLK), :],
                dst_ref=kv_buf.at[:, pl.ds(slot * BLK, BLK), :],
                send_sem=hs_sem.at[index],
                recv_sem=hr_sem.at[index],
                device_id={"tm": to},
                device_id_type=MESH,
            )

        near_beyond = near_copy(0, 0, 1, beyond)
        near_partner = near_copy(1, 2, 5, partner)
        far_partner = far_copy(2, 6, partner)
        backs = [
            pltpu.make_async_remote_copy(
                src_ref=source,
                dst_ref=target,
                send_sem=hs_sem.at[index],
                recv_sem=hr_sem.at[index],
                device_id={"tm": beyond},
                device_id_type=MESH,
            )
            for index, source, target in ((3, back_buf, got_buf), (4, back_lse, got_lse))
        ]

        pl.semaphore_wait(barrier, stems + has_beyond.astype(jnp.int32))
        pl.when(has_beyond)(near_beyond.start)
        near_partner.start()

        @pl.when(jnp.logical_not(has_beyond))
        def _():
            x_buf[BLK : 2 * BLK, :] = jnp.zeros((BLK, width), BF16)
            got_buf[...] = jnp.zeros((BLK, hw), BF16)
            got_lse[...] = jnp.full((8, BLK), NEG, F32)

        row = lax.broadcasted_iota(jnp.int32, (256, 256), 0)
        col = lax.broadcasted_iota(jnp.int32, (256, 256), 1)
        diag[...] = jnp.where((row >> 6) == (col >> 6), 1.0 / HD, 0.0).astype(BF16)

        loads[2].wait()
        loads[3].wait()
        for i, g in enumerate((g1, g2)):
            two = jnp.concatenate([g[...], g[...]], axis=1)
            wide = jnp.concatenate([two] * pairs, axis=1)
            gains[2 * i : 2 * i + 1, :] = wide[0:1] * (HD ** -0.5)
            gains[2 * i + 1 : 2 * i + 2, :] = wide[1:2]

        def normed(values, shift, scale):
            values = values.astype(F32)
            centred = values - jnp.mean(values, axis=-1, keepdims=True)
            var = jnp.mean(centred * centred, axis=-1, keepdims=True)
            return (centred * lax.rsqrt(var + EPS) * scale + shift).astype(BF16)

        def head_norm(values, gain):
            square = (values * values).astype(BF16)
            mean = jnp.concatenate(
                [matmul(square[:, i : i + 256], diag[...]) for i in range(0, hw, 256)], axis=1
            )
            return (values * lax.rsqrt(mean + EPS) * gain).astype(BF16)

        loads[0].wait()
        loads[1].wait()
        t_own = t_smem[me_s]

        def mods(which, at):
            return mod_buf[which, pl.ds(at, 1), :]

        shift1, scale1 = mods(0, t_own), mods(1, t_own) + 1.0

        def norm_blocks(first, last):
            def one(block, carry):
                for i in range(BLK // 16):
                    at = pl.ds(pl.multiple_of(block * BLK + i * 16, 16), 16)
                    norm_buf[at, :] = normed(x_buf[at, :], shift1, scale1)
                return carry

            lax.fori_loop(first, last, one, 0)

        def key_values(block):
            at = pl.ds(block * BLK, BLK)
            keys = matmul(norm_buf[at, :], w1[:, hw : 2 * hw])
            kv_buf[0, at, :] = head_norm(keys, gains[1:2, :])
            kv_buf[1, at, :] = matmul(norm_buf[at, :], w1[:, 2 * hw :]).astype(BF16)

        for load in own_loads:
            load.wait()
        norm_blocks(2, 5)
        loads[4].wait()
        key_values(3)
        key_values(2)
        far_partner.start()
        key_values(4)

        def queries(block):
            at = pl.ds((2 + block) * BLK, BLK)
            q_buf[pl.ds((1 + block) * BLK, BLK), :] = head_norm(
                matmul(norm_buf[at, :], w1[:, :hw]), gains[0:1, :]
            )

        for block in range(blocks):
            queries(block)

        r_at = lax.broadcasted_iota(jnp.int32, (2 * BLK, BLK), 0) & (BLK - 1)
        c_at = lax.broadcasted_iota(jnp.int32, (2 * BLK, BLK), 1)
        low_lanes = lax.broadcasted_iota(jnp.int32, (BLK, 128), 1) < HD
        bias = jnp.where(has_beyond, 0.0, NEG).astype(F32)
        slope = (c_at - r_at) * (1 - 2 * odd)

        def two_heads(q):
            zero = jnp.zeros_like(q)
            return jnp.concatenate(
                [jnp.where(low_lanes, q, zero), jnp.where(low_lanes, zero, q)], axis=0
            )

        def with_ones(v):
            return jnp.concatenate([v, jnp.ones_like(v)], axis=1)

        def pieces(block, pair, first, last):
            lanes = pl.ds(pair * 128, 128)
            at = pl.ds(first * BLK, (last - first) * BLK)
            q2 = two_heads(q_buf[pl.ds((1 + block) * BLK, BLK), lanes])
            scores = matmul_nt(q2, kv_buf[0, at, lanes])
            parts = []
            for slot in range(first, last):
                piece = scores[:, (slot - first) * BLK : (slot - first + 1) * BLK]
                if slot == block:
                    piece = jnp.where(slope >= 0, piece, NEG)
                if slot == block + 4:
                    piece = jnp.where(slope <= 0, piece, NEG)
                if slot < 2:
                    piece = piece + bias
                parts.append(piece)
            return jnp.concatenate(parts, axis=1), with_ones(kv_buf[1, at, lanes])

        lane = lax.broadcasted_iota(jnp.int32, (BLK, 128), 1)

        def heads(values):
            return jnp.where(low_lanes, values[:BLK], values[BLK:])

        def finish(pair, total, into):
            mixed = total[:, :128] / total[:, 128:]
            into[:, pl.ds(pair * 128, 128)] = heads(mixed).astype(BF16)

        def attend(block, first, last):
            for pair in range(pairs):
                scores, values = pieces(block, pair, first, last)
                top = jnp.max(scores, axis=-1, keepdims=True)
                total = matmul(jnp.exp(scores - top).astype(BF16), values)
                if block == 2:
                    finish(pair, total, attn_buf)
                elif block == 1:
                    m_buf[pair] = jnp.broadcast_to(top, (2 * BLK, 128))
                    o_buf[pair] = total
                else:
                    e_buf[pair, 0] = heads(jnp.broadcast_to(top, (2 * BLK, 128)))
                    e_buf[pair, 1] = heads(total[:, :128])
                    e_buf[pair, 2] = heads(total[:, 128:])

        def attend_more():
            for pair in range(pairs):
                scores, values = pieces(1, pair, 1, 2)
                before = m_buf[pair][:, 0:1]
                top = jnp.maximum(before, jnp.max(scores, axis=-1, keepdims=True))
                total = matmul(jnp.exp(scores - top).astype(BF16), values)
                finish(pair, total + o_buf[pair] * jnp.exp(before - top), attn_buf)

        def attend_back():
            stats = jnp.zeros((BLK, 128), F32)
            for pair in range(pairs):
                scores, values = pieces(-1, pair, 3, 4)
                top = jnp.max(scores, axis=-1, keepdims=True)
                total = matmul(jnp.exp(scores - top).astype(BF16), values)
                finish(pair, total, back_buf)
                lse = top + jnp.log(total[:, 128:])
                stats = jnp.where(lane == 2 * pair, lse[:BLK], stats)
                stats = jnp.where(lane == 2 * pair + 1, lse[BLK:], stats)
            back_lse[...] = jnp.transpose(stats)[:8, :]

        def attend_got():
            filler = jnp.zeros((BLK - 8, BLK), F32)
            stats = jnp.transpose(jnp.concatenate([got_lse[...], filler], axis=0))
            for pair in range(pairs):
                lanes = pl.ds(pair * 128, 128)
                lse = jnp.where(
                    low_lanes, stats[:, 2 * pair : 2 * pair + 1], stats[:, 2 * pair + 1 : 2 * pair + 2]
                )
                before = e_buf[pair, 0]
                top = jnp.maximum(before, lse)
                own, other = jnp.exp(before - top), jnp.exp(lse - top)
                mixed = e_buf[pair, 1] * own + got_buf[:, lanes].astype(F32) * other
                attn_buf[:, lanes] = (mixed / (e_buf[pair, 2] * own + other)).astype(BF16)

        gate1 = mods(2, t_own)

        def first_copy(block, r):
            return pltpu.make_async_remote_copy(
                src_ref=first_buf.at[block, peers[r]],
                dst_ref=recv_buf.at[block, me_s],
                send_sem=as_sem.at[block, r],
                recv_sem=ar_sem.at[block, r],
                device_id={"stem": peers[r]},
                device_id_type=MESH,
            )

        def home_copy(block, r):
            return pltpu.make_async_remote_copy(
                src_ref=cmix_buf.at[block, peers[r]],
                dst_ref=recv2_buf.at[block, me_s],
                send_sem=bs_sem.at[block, r],
                recv_sem=br_sem.at[block, r],
                device_id={"stem": peers[r]},
                device_id_type=MESH,
            )

        def first_part(block):
            at = pl.ds((2 + block) * BLK, BLK)
            value = x_buf[at, :].astype(F32) + gate1 * matmul(attn_buf[...], wo1[...])
            first_buf[block] = value.astype(BF16).reshape(stems, part, width)
            recv_buf[block, me_s] = first_buf[block, me_s]
            for r in order:
                first_copy(block, r).start()

        def cross_part(block):
            for r in order:
                first_copy(block, r).wait_recv()
            for s in range(stems):
                norm_buf[s * part : (s + 1) * part, :] = normed(
                    recv_buf[block, s], mods(3, t_smem[s]), mods(4, t_smem[s]) + 1.0
                )
            rows_in = norm_buf[0:BLK, :]
            q = head_norm(matmul(rows_in, w2[:, :hw]), gains[2:3, :])
            k = head_norm(matmul(rows_in, w2[:, hw : 2 * hw]), gains[3:4, :])
            v = matmul(rows_in, w2[:, 2 * hw :]).astype(BF16)
            same = (r_at & (part - 1)) == (c_at & (part - 1))
            for pair in range(pairs):
                lanes = slice(pair * 128, pair * 128 + 128)
                scores = jnp.where(same, matmul_nt(two_heads(q[:, lanes]), k[:, lanes]), NEG)
                top = jnp.max(scores, axis=-1, keepdims=True)
                raised = jnp.exp(scores - top).astype(BF16)
                total = matmul(raised, with_ones(v[:, lanes]))
                mixed = total[:, :128] / total[:, 128:]
                both = jnp.where(low_lanes, mixed[:BLK], mixed[BLK:]).astype(BF16)
                cmix_buf[block, :, :, lanes] = both.reshape(stems, part, 128)
            recv2_buf[block, me_s] = cmix_buf[block, me_s]

        def send_home(block):
            for r in order:
                home_copy(block, r).start()

        gate2 = mods(5, t_own)

        def last_part(block):
            for r in order:
                home_copy(block, r).wait_recv()
            cross = matmul(recv2_buf[block].reshape(BLK, hw), wo2[...]).astype(BF16).astype(F32)
            first = first_buf[block].reshape(BLK, width).astype(F32)
            out_buf[pl.ds(block * BLK, BLK), :] = (first + gate2 * cross).astype(BF16)
            store(block).start()

        def store(block):
            at = pl.ds(block * BLK, BLK)
            return pltpu.make_async_copy(
                out_buf.at[at, :], out_hbm.at[rows_of(block), :], store_sem.at[block]
            )

        near_partner.wait_recv()
        norm_blocks(5, 6)
        key_values(5)
        far_partner.wait_recv()
        attend(2, 2, 7)
        loads[5].wait()
        first_part(2)
        attend(1, 2, 6)
        pl.when(has_beyond)(near_beyond.wait_recv)
        norm_blocks(1, 2)
        queries(-1)
        attend_back()
        key_values(1)
        for back in backs:
            pl.when(has_beyond)(back.start)
        attend_more()
        first_part(1)
        attend(0, 1, 5)
        loads[6].wait()
        cross_part(2)
        for back in backs:
            pl.when(has_beyond)(back.wait_recv)
        attend_got()
        first_part(0)
        send_home(2)
        cross_part(1)
        send_home(1)
        loads[7].wait()
        last_part(2)
        cross_part(0)
        send_home(0)
        last_part(1)
        last_part(0)

        pl.when(has_beyond)(near_beyond.wait_send)
        for back in backs:
            pl.when(has_beyond)(back.wait_send)
        near_partner.wait_send()
        far_partner.wait_send()
        for block in (1, 0, 2):
            for r in order:
                first_copy(block, r).wait_send()
                home_copy(block, r).wait_send()
            store(block).wait()

    return kernel


def solution(mesh):
    stems, tms = mesh.shape["stem"], mesh.shape["tm"]

    def on_device(
        frames, timestep, modulation, qkv_self, out_self, gain_self, qkv_cross, out_cross, gain_cross
    ):
        rows, width = frames.shape[1:]
        hw = out_self.shape[0]
        steps = modulation.shape[0]
        blocks, part, pairs = rows // BLK, BLK // stems, hw // 128
        result = pl.pallas_call(
            make_kernel(stems, tms, steps, rows, width, hw),
            out_shape=jax.ShapeDtypeStruct((rows, width), BF16),
            in_specs=[pl.BlockSpec(memory_space=pltpu.HBM)] * 9,
            out_specs=pl.BlockSpec(memory_space=pl.ANY),
            scratch_shapes=[
                pltpu.VMEM((rows + 4 * BLK, width), BF16),
                pltpu.SMEM((stems,), jnp.int32),
                pltpu.VMEM((6, steps, width), F32),
                pltpu.VMEM((width, 3 * hw), BF16),
                pltpu.VMEM((hw, width), BF16),
                pltpu.VMEM((2, HD), F32),
                pltpu.VMEM((width, 3 * hw), BF16),
                pltpu.VMEM((hw, width), BF16),
                pltpu.VMEM((2, HD), F32),
                pltpu.VMEM((4, hw), F32),
                pltpu.VMEM((256, 256), BF16),
                pltpu.VMEM((rows + 4 * BLK, width), BF16),
                pltpu.VMEM((rows + BLK, hw), BF16),
                pltpu.VMEM((2, rows + 4 * BLK, hw), BF16),
                pltpu.VMEM((pairs, 2 * BLK, 128), F32),
                pltpu.VMEM((pairs, 2 * BLK, 256), F32),
                pltpu.VMEM((pairs, 3, BLK, 128), F32),
                pltpu.VMEM((BLK, hw), BF16),
                pltpu.VMEM((BLK, hw), BF16),
                pltpu.VMEM((BLK, hw), BF16),
                pltpu.VMEM((8, BLK), F32),
                pltpu.VMEM((8, BLK), F32),
                pltpu.VMEM((blocks, stems, part, width), BF16),
                pltpu.VMEM((blocks, stems, part, width), BF16),
                pltpu.VMEM((blocks, stems, part, hw), BF16),
                pltpu.VMEM((blocks, stems, part, hw), BF16),
                pltpu.VMEM((rows, width), BF16),
                pltpu.SemaphoreType.DMA((8 + blocks,)),
                pltpu.SemaphoreType.DMA((blocks,)),
                pltpu.SemaphoreType.DMA((5,)),
                pltpu.SemaphoreType.DMA((5,)),
                pltpu.SemaphoreType.DMA((blocks, stems)),
                pltpu.SemaphoreType.DMA((blocks, stems)),
                pltpu.SemaphoreType.DMA((blocks, stems)),
                pltpu.SemaphoreType.DMA((blocks, stems)),
            ],
            compiler_params=pltpu.CompilerParams(
                collective_id=0, has_side_effects=True, vmem_limit_bytes=36 << 20
            ),
            name="block",
        )(
            *(
                pltpu.with_memory_space_constraint(value, pltpu.HBM)
                for value in (
                    frames.reshape(rows, width), timestep, modulation.transpose(1, 0, 2),
                    qkv_self, out_self, gain_self, qkv_cross, out_cross, gain_cross,
                )
            )
        )
        return result[None]

    return jax.shard_map(
        on_device,
        mesh=mesh,
        in_specs=(P("stem", "tm", None), P(), P(), P(), P(), P(), P(), P(), P()),
        out_specs=P("stem", "tm", None),
        check_vma=False,
    )
```

time: 44.5 us -> 40 us (0.90); the launches traced: 44.4 us -> 39.3 us
  Pallas kernels: 42.3 us -> 38.4 us
  local copies, waits for them, and re-layouts: 2.06 us -> 0.88 us
    pallas_call x1, Pallas kernels: 42.3 us -> 38.4 us  [on_device(): pl.pallas_call(make_kernel(stems, tms, steps, rows, width, hw), out_shape...]
    unnamed x1, local copies, waits for them, and re-layouts: 2.06 us -> 0.88 us
where the time goes in v2:
time: 40 us; the launch traced here: 39.3 us
  Pallas kernels  38.4 us (96%)
  local copies, waits for them, and re-layouts  0.88 us (2%)
    pallas_call x1, Pallas kernels, on_device(): pl.pallas_call(make_kernel(stems, tms, steps, rows, width, hw), out_shape...  38.4 us
    unnamed x1, local copies, waits for them, and re-layouts  0.88 us

profile of v2, /device:TPU:6, one launch (start us, length us, event | category | flops | bytes accessed | tf_op | source)
XLA Modules:
  0.0 39.3 jit_solution(10193992178751280994)
XLA Ops:
  0.0 38.4 %block.1 = bf16[384,1024]{1,0:T(8,128)(2,1)S(1)} custom-call(bf16[384,1024]{1,0:T(8,128)(2,1)} %bitcast.5, s32[8]{0:T(128)} %timestep_hbm.1, f32[6,50,1024]{2,1,0:T(8,128)} %bitcast.4, bf16[1024,1536]{1,0:T(8,128)(2,1)} %w1_hbm.1, bf16[512,1024]{1,0:T(8,128)(2,1)} %wo1_hbm.1, f32[2,64]{1,0:T(2,128)} %g1_hbm.1, bf16[1024,1536]{1,0:T(8,128)(2,1)} %w2_hbm.1, ...), custom_call_target="tpu_custom_call" | custom-call | tf_op jit(solution)/shard_map/block/pallas_call | solution.py:424
  38.4 0.9 %copy.11 = bf16[1,384,1024]{2,1,0:T(8,128)(2,1)} copy(bf16[1,384,1024]{2,1,0:T(8,128)(2,1)S(1)} %bitcast.3) | data formatting | bytes 1572864

commit v3 on v2

--- a/solution.py
+++ b/solution.py
@@ -29,11 +29,11 @@
 
     def kernel(
         frames_hbm, timestep_hbm, mod_hbm, w1_hbm, wo1_hbm, g1_hbm, w2_hbm, wo2_hbm, g2_hbm,
-        out_hbm,
+        out_ref,
         x_buf, t_smem, mod_buf, w1, wo1, g1, w2, wo2, g2, gains, diag,
         norm_buf, q_buf, kv_buf, m_buf, o_buf, e_buf, attn_buf, back_buf, got_buf, back_lse, got_lse,
-        first_buf, recv_buf, cmix_buf, recv2_buf, out_buf,
-        load_sem, store_sem, hs_sem, hr_sem, as_sem, ar_sem, bs_sem, br_sem,
+        first_buf, recv_buf, cmix_buf, recv2_buf,
+        load_sem, hs_sem, hr_sem, as_sem, ar_sem, bs_sem, br_sem,
     ):
         me_s = lax.axis_index("stem")
         me_t = lax.axis_index("tm")
@@ -45,13 +45,30 @@
             place = block + odd * (blocks - 1 - 2 * block)
             return pl.ds(pl.multiple_of(place * BLK, BLK), BLK)
 
-        half = stems // 2
+        half, fold = stems // 2, BLK // 2
+
+        def chunk_of(stem):
+            hi, lo = stem // half, lax.rem(stem, half)
+            return half * (1 - lo // 2) + 2 * hi + lax.rem(lo, 2)
+
         me_hi, me_lo = me_s // half, lax.rem(me_s, half)
-        peers = [
-            lax.rem(me_hi + r // half, 2) * half + lax.rem(me_lo + r % half, half)
-            for r in range(stems)
-        ]
-        order = list(range(half, stems)) + list(range(1, half))
+
+        def shifted(r, sign):
+            hi = lax.rem(me_hi + r // half, 2)
+            return hi * half + lax.rem(me_lo + half + sign * (r % half), half)
+
+        peers = [shifted(r, 1) for r in range(stems)]
+        sources = [shifted(r, -1) for r in range(stems)]
+        near_side, far_side = [2, 1, 3], [6, 5, 7, 4]
+        order = far_side + near_side
+
+        def others(action, which=None):
+            for r in order:
+                if which is None:
+                    action(r)
+                else:
+                    in_first = lax.rem(peers[r], half) < half // 2
+                    pl.when(in_first == (which == 1))(lambda r=r: action(r))
 
         loads = [
             pltpu.make_async_copy(src, dst, load_sem.at[i])
@@ -65,9 +82,7 @@
         def greet(to):
             pl.semaphore_signal(barrier, inc=1, device_id=to, device_id_type=MESH)
 
-        for r in order:
-            greet({"stem": peers[r]})
-
+        others(lambda r: greet({"stem": peers[r]}))
         greet({"tm": partner})
 
         @pl.when(has_beyond)
@@ -88,10 +103,11 @@
         for load in loads[1:]:
             load.start()
 
-        def near_copy(index, block, slot, to):
+        def near_copy(index, block, slot, to, skip=0, size=BLK):
+            place = block + odd * (blocks - 1 - 2 * block)
             return pltpu.make_async_remote_copy(
-                src_ref=frames_hbm.at[rows_of(block), :],
-                dst_ref=x_buf.at[pl.ds(slot * BLK, BLK), :],
+                src_ref=frames_hbm.at[pl.ds(pl.multiple_of(place * BLK + skip, 16), size), :],
+                dst_ref=x_buf.at[pl.ds(slot * BLK + skip, size), :],
                 send_sem=hs_sem.at[index],
                 recv_sem=hr_sem.at[index],
                 device_id={"tm": to},
@@ -108,30 +124,37 @@
                 device_id_type=MESH,
             )
 
-        near_beyond = near_copy(0, 0, 1, beyond)
-        near_partner = near_copy(1, 2, 5, partner)
-        far_partner = far_copy(2, 6, partner)
+        near_beyond = [near_copy(h, 0, 1, beyond, h * fold, fold) for h in range(2)]
+        near_partner = near_copy(2, 2, 5, partner)
+        far_partner = far_copy(3, 6, partner)
         backs = [
-            pltpu.make_async_remote_copy(
-                src_ref=source,
-                dst_ref=target,
-                send_sem=hs_sem.at[index],
-                recv_sem=hr_sem.at[index],
-                device_id={"tm": beyond},
-                device_id_type=MESH,
-            )
-            for index, source, target in ((3, back_buf, got_buf), (4, back_lse, got_lse))
+            [
+                pltpu.make_async_remote_copy(
+                    src_ref=source,
+                    dst_ref=target,
+                    send_sem=hs_sem.at[index],
+                    recv_sem=hr_sem.at[index],
+                    device_id={"tm": beyond},
+                    device_id_type=MESH,
+                )
+                for index, source, target in (
+                    (4 + h, back_buf.at[pl.ds(h * fold, fold), :], got_buf.at[pl.ds(h * fold, fold), :]),
+                    (6 + h, back_lse.at[h], got_lse.at[h]),
+                )
+            ]
+            for h in range(2)
         ]
 
         pl.semaphore_wait(barrier, stems + has_beyond.astype(jnp.int32))
-        pl.when(has_beyond)(near_beyond.start)
+        pl.when(has_beyond)(near_beyond[1].start)
+        pl.when(has_beyond)(near_beyond[0].start)
         near_partner.start()
 
         @pl.when(jnp.logical_not(has_beyond))
         def _():
             x_buf[BLK : 2 * BLK, :] = jnp.zeros((BLK, width), BF16)
             got_buf[...] = jnp.zeros((BLK, hw), BF16)
-            got_lse[...] = jnp.full((8, BLK), NEG, F32)
+            got_lse[...] = jnp.full((2, 8, BLK), NEG, F32)
 
         row = lax.broadcasted_iota(jnp.int32, (256, 256), 0)
         col = lax.broadcasted_iota(jnp.int32, (256, 256), 1)
@@ -175,6 +198,11 @@
                 return carry
 
             lax.fori_loop(first, last, one, 0)
+
+        def norm_half(h):
+            for i in range(fold // 16):
+                at = pl.ds(BLK + h * fold + i * 16, 16)
+                norm_buf[at, :] = normed(x_buf[at, :], shift1, scale1)
 
         def key_values(block):
             at = pl.ds(block * BLK, BLK)
@@ -197,6 +225,11 @@
                 matmul(norm_buf[at, :], w1[:, :hw]), gains[0:1, :]
             )
 
+        def queries_half(h):
+            q_buf[pl.ds(h * fold, fold), :] = head_norm(
+                matmul(norm_buf[pl.ds(BLK + h * fold, fold), :], w1[:, :hw]), gains[0:1, :]
+            )
+
         for block in range(blocks):
             queries(block)
 
@@ -207,10 +240,8 @@
         slope = (c_at - r_at) * (1 - 2 * odd)
 
         def two_heads(q):
-            zero = jnp.zeros_like(q)
-            return jnp.concatenate(
-                [jnp.where(low_lanes, q, zero), jnp.where(low_lanes, zero, q)], axis=0
-            )
+            zero, low = jnp.zeros_like(q), low_lanes[: q.shape[0]]
+            return jnp.concatenate([jnp.where(low, q, zero), jnp.where(low, zero, q)], axis=0)
 
         def with_ones(v):
             return jnp.concatenate([v, jnp.ones_like(v)], axis=1)
@@ -235,11 +266,12 @@
         lane = lax.broadcasted_iota(jnp.int32, (BLK, 128), 1)
 
         def heads(values):
-            return jnp.where(low_lanes, values[:BLK], values[BLK:])
-
-        def finish(pair, total, into):
+            n = values.shape[0] // 2
+            return jnp.where(low_lanes[:n], values[:n], values[n:])
+
+        def finish(pair, total, into, rows_at=slice(None)):
             mixed = total[:, :128] / total[:, 128:]
-            into[:, pl.ds(pair * 128, 128)] = heads(mixed).astype(BF16)
+            into[rows_at, pl.ds(pair * 128, 128)] = heads(mixed).astype(BF16)
 
         def attend(block, first, last):
             for pair in range(pairs):
@@ -264,69 +296,87 @@
                 total = matmul(jnp.exp(scores - top).astype(BF16), values)
                 finish(pair, total + o_buf[pair] * jnp.exp(before - top), attn_buf)
 
-        def attend_back():
-            stats = jnp.zeros((BLK, 128), F32)
+        def attend_back(h):
+            stats = jnp.zeros((fold, 128), F32)
+            at, keys = pl.ds(h * fold, fold), pl.ds(3 * BLK, BLK)
+            r_half = (lax.broadcasted_iota(jnp.int32, (BLK, BLK), 0) & (fold - 1)) + h * fold
+            tilt = (c_at[:BLK] - r_half) * (1 - 2 * odd)
             for pair in range(pairs):
-                scores, values = pieces(-1, pair, 3, 4)
+                lanes = pl.ds(pair * 128, 128)
+                scores = matmul_nt(two_heads(q_buf[at, lanes]), kv_buf[0, keys, lanes])
+                scores = jnp.where(tilt <= 0, scores, NEG)
                 top = jnp.max(scores, axis=-1, keepdims=True)
-                total = matmul(jnp.exp(scores - top).astype(BF16), values)
-                finish(pair, total, back_buf)
+                total = matmul(jnp.exp(scores - top).astype(BF16), with_ones(kv_buf[1, keys, lanes]))
+                finish(pair, total, back_buf, at)
                 lse = top + jnp.log(total[:, 128:])
-                stats = jnp.where(lane == 2 * pair, lse[:BLK], stats)
-                stats = jnp.where(lane == 2 * pair + 1, lse[BLK:], stats)
-            back_lse[...] = jnp.transpose(stats)[:8, :]
-
-        def attend_got():
+                stats = jnp.where(lane[:fold] == 2 * pair, lse[:fold], stats)
+                stats = jnp.where(lane[:fold] == 2 * pair + 1, lse[fold:], stats)
+            filler = jnp.zeros((BLK - fold, 128), F32)
+            back_lse[h] = jnp.transpose(jnp.concatenate([stats, filler], axis=0))[:8, :]
+
+        def attend_got(h):
+            at = pl.ds(h * fold, fold)
             filler = jnp.zeros((BLK - 8, BLK), F32)
-            stats = jnp.transpose(jnp.concatenate([got_lse[...], filler], axis=0))
+            stats = jnp.transpose(jnp.concatenate([got_lse[h], filler], axis=0))[:fold]
             for pair in range(pairs):
                 lanes = pl.ds(pair * 128, 128)
                 lse = jnp.where(
-                    low_lanes, stats[:, 2 * pair : 2 * pair + 1], stats[:, 2 * pair + 1 : 2 * pair + 2]
+                    low_lanes[:fold],
+                    stats[:, 2 * pair : 2 * pair + 1],
+                    stats[:, 2 * pair + 1 : 2 * pair + 2],
                 )
-                before = e_buf[pair, 0]
+                before = e_buf[pair, 0, at, :]
                 top = jnp.maximum(before, lse)
                 own, other = jnp.exp(before - top), jnp.exp(lse - top)
-                mixed = e_buf[pair, 1] * own + got_buf[:, lanes].astype(F32) * other
-                attn_buf[:, lanes] = (mixed / (e_buf[pair, 2] * own + other)).astype(BF16)
+                mixed = e_buf[pair, 1, at, :] * own + got_buf[at, lanes].astype(F32) * other
+                attn_buf[at, lanes] = (mixed / (e_buf[pair, 2, at, :] * own + other)).astype(BF16)
 
         gate1 = mods(2, t_own)
 
-        def first_copy(block, r):
+        def first_copy(block, r, source):
             return pltpu.make_async_remote_copy(
-                src_ref=first_buf.at[block, peers[r]],
-                dst_ref=recv_buf.at[block, me_s],
+                src_ref=first_buf.at[block, chunk_of(peers[r])],
+                dst_ref=recv_buf.at[block, source],
                 send_sem=as_sem.at[block, r],
                 recv_sem=ar_sem.at[block, r],
                 device_id={"stem": peers[r]},
                 device_id_type=MESH,
             )
 
-        def home_copy(block, r):
+        def home_copy(block, r, source):
             return pltpu.make_async_remote_copy(
                 src_ref=cmix_buf.at[block, peers[r]],
-                dst_ref=recv2_buf.at[block, me_s],
+                dst_ref=recv2_buf.at[block, chunk_of(source)],
                 send_sem=bs_sem.at[block, r],
                 recv_sem=br_sem.at[block, r],
                 device_id={"stem": peers[r]},
                 device_id_type=MESH,
             )
 
-        def first_part(block):
-            at = pl.ds((2 + block) * BLK, BLK)
-            value = x_buf[at, :].astype(F32) + gate1 * matmul(attn_buf[...], wo1[...])
-            first_buf[block] = value.astype(BF16).reshape(stems, part, width)
-            recv_buf[block, me_s] = first_buf[block, me_s]
-            for r in order:
-                first_copy(block, r).start()
+        def first_part(block, skip=0, size=BLK):
+            at = pl.ds((2 + block) * BLK + skip, size)
+            value = x_buf[at, :].astype(F32) + gate1 * matmul(attn_buf[pl.ds(skip, size), :], wo1[...])
+            first_buf[block, pl.ds(skip // part, size // part)] = value.astype(BF16).reshape(
+                size // part, part, width
+            )
+
+        def send_first(block, which=None):
+            others(lambda r: first_copy(block, r, me_s).start(), which)
+
+        def keep_first(block):
+            recv_buf[block, me_s] = first_buf[block, chunk_of(me_s)]
 
         def cross_part(block):
-            for r in order:
-                first_copy(block, r).wait_recv()
-            for s in range(stems):
-                norm_buf[s * part : (s + 1) * part, :] = normed(
-                    recv_buf[block, s], mods(3, t_smem[s]), mods(4, t_smem[s]) + 1.0
-                )
+            for group in ([0] + near_side, far_side):
+                for r in group:
+                    if r:
+                        first_copy(block, r, sources[r]).wait_recv()
+                for r in group:
+                    s = sources[r]
+                    at = pl.ds(pl.multiple_of(s * part, part), part)
+                    norm_buf[at, :] = normed(
+                        recv_buf[block, s], mods(3, t_smem[s]), mods(4, t_smem[s]) + 1.0
+                    )
             rows_in = norm_buf[0:BLK, :]
             q = head_norm(matmul(rows_in, w2[:, :hw]), gains[2:3, :])
             k = head_norm(matmul(rows_in, w2[:, hw : 2 * hw]), gains[3:4, :])
@@ -341,27 +391,18 @@
                 mixed = total[:, :128] / total[:, 128:]
                 both = jnp.where(low_lanes, mixed[:BLK], mixed[BLK:]).astype(BF16)
                 cmix_buf[block, :, :, lanes] = both.reshape(stems, part, 128)
-            recv2_buf[block, me_s] = cmix_buf[block, me_s]
+            recv2_buf[block, chunk_of(me_s)] = cmix_buf[block, me_s]
 
         def send_home(block):
-            for r in order:
-                home_copy(block, r).start()
+            others(lambda r: home_copy(block, r, me_s).start())
 
         gate2 = mods(5, t_own)
 
         def last_part(block):
-            for r in order:
-                home_copy(block, r).wait_recv()
+            others(lambda r: home_copy(block, r, sources[r]).wait_recv())
             cross = matmul(recv2_buf[block].reshape(BLK, hw), wo2[...]).astype(BF16).astype(F32)
             first = first_buf[block].reshape(BLK, width).astype(F32)
-            out_buf[pl.ds(block * BLK, BLK), :] = (first + gate2 * cross).astype(BF16)
-            store(block).start()
-
-        def store(block):
-            at = pl.ds(block * BLK, BLK)
-            return pltpu.make_async_copy(
-                out_buf.at[at, :], out_hbm.at[rows_of(block), :], store_sem.at[block]
-            )
+            out_ref[rows_of(block), :] = (first + gate2 * cross).astype(BF16)
 
         near_partner.wait_recv()
         norm_blocks(5, 6)
@@ -370,43 +411,49 @@
         attend(2, 2, 7)
         loads[5].wait()
         first_part(2)
-        attend(1, 2, 6)
-        pl.when(has_beyond)(near_beyond.wait_recv)
-        norm_blocks(1, 2)
-        queries(-1)
-        attend_back()
+        send_first(2)
+        keep_first(2)
+        for h in (1, 0):
+            pl.when(has_beyond)(near_beyond[h].wait_recv)
+            norm_half(h)
+            queries_half(h)
+            attend_back(h)
+            for back in backs[h]:
+                pl.when(has_beyond)(back.start)
+            if h:
+                attend(1, 2, 6)
         key_values(1)
-        for back in backs:
-            pl.when(has_beyond)(back.start)
         attend_more()
         first_part(1)
+        send_first(1)
+        keep_first(1)
         attend(0, 1, 5)
         loads[6].wait()
+        for h in (1, 0):
+            for back in backs[h]:
+                pl.when(has_beyond)(back.wait_recv)
+            attend_got(h)
+            first_part(0, h * fold, fold)
+            send_first(0, h)
+        keep_first(0)
         cross_part(2)
-        for back in backs:
-            pl.when(has_beyond)(back.wait_recv)
-        attend_got()
-        first_part(0)
         send_home(2)
         cross_part(1)
         send_home(1)
         loads[7].wait()
-        last_part(2)
         cross_part(0)
         send_home(0)
+        last_part(2)
         last_part(1)
         last_part(0)
 
-        pl.when(has_beyond)(near_beyond.wait_send)
-        for back in backs:
-            pl.when(has_beyond)(back.wait_send)
+        for copy in near_beyond + backs[0] + backs[1]:
+            pl.when(has_beyond)(copy.wait_send)
         near_partner.wait_send()
         far_partner.wait_send()
         for block in (1, 0, 2):
-            for r in order:
-                first_copy(block, r).wait_send()
-                home_copy(block, r).wait_send()
-            store(block).wait()
+            others(lambda r: first_copy(block, r, me_s).wait_send())
+            others(lambda r: home_copy(block, r, me_s).wait_send())
 
     return kernel
 
@@ -425,7 +472,7 @@
             make_kernel(stems, tms, steps, rows, width, hw),
             out_shape=jax.ShapeDtypeStruct((rows, width), BF16),
             in_specs=[pl.BlockSpec(memory_space=pltpu.HBM)] * 9,
-            out_specs=pl.BlockSpec(memory_space=pl.ANY),
+            out_specs=pl.BlockSpec(memory_space=pltpu.VMEM),
             scratch_shapes=[
                 pltpu.VMEM((rows + 4 * BLK, width), BF16),
                 pltpu.SMEM((stems,), jnp.int32),
@@ -447,17 +494,15 @@
                 pltpu.VMEM((BLK, hw), BF16),
                 pltpu.VMEM((BLK, hw), BF16),
                 pltpu.VMEM((BLK, hw), BF16),
-                pltpu.VMEM((8, BLK), F32),
-                pltpu.VMEM((8, BLK), F32),
+                pltpu.VMEM((2, 8, BLK), F32),
+                pltpu.VMEM((2, 8, BLK), F32),
                 pltpu.VMEM((blocks, stems, part, width), BF16),
                 pltpu.VMEM((blocks, stems, part, width), BF16),
                 pltpu.VMEM((blocks, stems, part, hw), BF16),
                 pltpu.VMEM((blocks, stems, part, hw), BF16),
-                pltpu.VMEM((rows, width), BF16),
                 pltpu.SemaphoreType.DMA((8 + blocks,)),
-                pltpu.SemaphoreType.DMA((blocks,)),
-                pltpu.SemaphoreType.DMA((5,)),
-                pltpu.SemaphoreType.DMA((5,)),
+                pltpu.SemaphoreType.DMA((8,)),
+                pltpu.SemaphoreType.DMA((8,)),
                 pltpu.SemaphoreType.DMA((blocks, stems)),
                 pltpu.SemaphoreType.DMA((blocks, stems)),
                 pltpu.SemaphoreType.DMA((blocks, stems)),

time: 40 us -> 38.1 us (0.953); the launches traced: 39.3 us -> 37.9 us
  Pallas kernels: 38.4 us -> 37 us
    pallas_call x1, Pallas kernels: 38.4 us -> 37 us  [on_device(): pl.pallas_call(make_kernel(stems, tms, steps, rows, width, hw), out_shape...]
where the time goes in v3:
time: 38.1 us; the launch traced here: 37.9 us
  Pallas kernels  37 us (97%)
  local copies, waits for them, and re-layouts  0.88 us (2%)
    pallas_call x1, Pallas kernels, on_device(): pl.pallas_call(make_kernel(stems, tms, steps, rows, width, hw), out_shape...  37 us
    unnamed x1, local copies, waits for them, and re-layouts  0.88 us

profile of v3, /device:TPU:6, one launch (start us, length us, event | category | flops | bytes accessed | tf_op | source)
XLA Modules:
  0.0 37.9 jit_solution(7088892384916273574)
XLA Ops:
  0.0 37.0 %block.1 = bf16[384,1024]{1,0:T(8,128)(2,1)S(1)} custom-call(bf16[384,1024]{1,0:T(8,128)(2,1)} %bitcast.5, s32[8]{0:T(128)} %timestep_hbm.1, f32[6,50,1024]{2,1,0:T(8,128)} %bitcast.4, bf16[1024,1536]{1,0:T(8,128)(2,1)} %w1_hbm.1, bf16[512,1024]{1,0:T(8,128)(2,1)} %wo1_hbm.1, f32[2,64]{1,0:T(2,128)} %g1_hbm.1, bf16[1024,1536]{1,0:T(8,128)(2,1)} %w2_hbm.1, ...), custom_call_target="tpu_custom_call" | custom-call | tf_op jit(solution)/shard_map/block/pallas_call | solution.py:471
  37.0 0.9 %copy.11 = bf16[1,384,1024]{2,1,0:T(8,128)(2,1)} copy(bf16[1,384,1024]{2,1,0:T(8,128)(2,1)S(1)} %bitcast.3) | data formatting | bytes 1572864
